TPU v7x, 32 devices: a whole 2x2x4 slice. The times are simulated.
32 devices in a mesh: grp: 2 (over y), band: 8 (over z, x), filt: 2 (over core).
Axes of the slice: x: 2, y: 2, z: 4, core: 2. Of those that a mesh axis runs over, the one named last changes fastest.
Arguments:
- coeff_maps: bfloat16 [128, 64, 512], P(('grp', 'filt'), 'band'), parts along dimension 0, may hold values from -0.75 to 0.75
- image: bfloat16 [6, 64, 512], P('grp', 'band'), parts along dimension 0, may hold values from -24 to 24
- target: bfloat16 [1024, 2, 3, 64, 64], P(('grp', 'band'), None, None, 'filt'), parts along dimension 0, may hold values from -1.5 to 1.5
- dual_rim: float32 [128, 768], P(('grp', 'filt')), parts along dimension 0, may hold values from -18 to 18, as said below
Outputs:
- dict_spectra: bfloat16 [1024, 2, 3, 64, 64], P(('grp', 'band'), None, None, 'filt'), parts along dimension 0
- dictionary: float32 [128, 768], P(('grp', 'filt')), parts along dimension 0
There are 2 independent parts, one for each index of `grp`. A program takes and returns all parts, laid end to end along the dimension named above; each array names one. Nothing has to cross between parts.
Inputs may be any that keep to these rules, and one draw needn't show every extreme that they name: `dual_rim`: a scaled dual variable on the filters' support.
All inputs are finite; a program needn't handle non-finite values.
Results may differ from a plain program's by a relative error of at most 0.0059.
Values may be sent and summed in bfloat16 or wider, within the bound.
No kernel may reach another device: no remote copies, remote signals or barrier semaphores. Data moves between devices by JAX's collectives and lax.ppermute only.
A program may use at most 128 MiB of HBM per device.

v0:
```python
import math
import jax
import jax.numpy as jnp
from jax import lax
from jax.sharding import PartitionSpec as P

K = 16
penalty = 1.0


def forward_columns(length):
    ramp = jnp.arange(length, dtype=jnp.int32)
    phases = ramp[:, None] * ramp[None, :] % length
    angles = phases.astype(jnp.float32) * (2.0 * math.pi / length)
    factor = 1.0 / math.sqrt(length)
    lookup = jnp.stack([jnp.cos(angles) * factor, -jnp.sin(angles) * factor], axis=2)
    return lookup.reshape(length, 2 * length).astype(jnp.bfloat16)


def forward_rows(length):
    ramp = jnp.arange(length, dtype=jnp.int32)
    phases = ramp[:, None] * ramp[None, :] % length
    angles = phases.astype(jnp.float32) * (2.0 * math.pi / length)
    factor = 1.0 / math.sqrt(length)
    return jnp.stack([jnp.cos(angles) * factor, jnp.sin(angles) * factor], axis=0).astype(
        jnp.bfloat16
    )


def inverse_rows(length, width):
    ramp = jnp.arange(length, dtype=jnp.int32)
    reach = jnp.arange(width, dtype=jnp.int32)
    phases = ramp[:, None] * reach[None, :] % length
    angles = phases.astype(jnp.float32) * (2.0 * math.pi / length)
    factor = 1.0 / math.sqrt(length)
    return jnp.stack([jnp.cos(angles) * factor, jnp.sin(angles) * factor], axis=1)


def inverse_columns(length, total_cols, width):
    freqs = jnp.arange(length, dtype=jnp.int32)
    reach = jnp.arange(width, dtype=jnp.int32)
    phases = freqs[:, None] * reach[None, :] % total_cols
    angles = phases.astype(jnp.float32) * (2.0 * math.pi / total_cols)
    factor = 1.0 / math.sqrt(total_cols)
    return jnp.stack([jnp.cos(angles) * factor, jnp.sin(angles) * factor], axis=1)


def spectra(slab_rows, lookup, freqs, members):
    height = slab_rows.shape[0]
    products = jnp.einsum("hk,tgh->ktg", slab_rows, lookup, preferred_element_type=jnp.float32)
    products = products.reshape(freqs, 2, members, 2, height)
    real_part = products[:, 0, :, 0] + products[:, 1, :, 1]
    imag_part = products[:, 1, :, 0] - products[:, 0, :, 1]
    return (real_part, imag_part)


def body(coeff_maps, image, target, dual_rim):
    filters, band_rows, width_cols = coeff_maps.shape
    channels = image.shape[0]
    band_count = lax.axis_size("band")
    height = band_rows * band_count
    per_band = width_cols // band_count
    col_lookup = forward_columns(width_cols)
    row_lookup = forward_rows(height)
    col_maps = jnp.einsum("mrn,nk->rkm", coeff_maps, col_lookup, preferred_element_type=jnp.float32)
    col_maps = col_maps.astype(jnp.bfloat16).reshape(band_rows, 2 * width_cols * filters)
    col_image = jnp.einsum("crn,nk->rkc", image, col_lookup, preferred_element_type=jnp.float32)
    col_image = col_image.astype(jnp.bfloat16).reshape(band_rows, 2 * width_cols * channels)
    got_maps, got_image = (
        lax.all_to_all(col_maps, "band", split_axis=1, concat_axis=0, tiled=True),
        lax.all_to_all(col_image, "band", split_axis=1, concat_axis=0, tiled=True),
    )
    x_re, x_im = spectra(got_maps, row_lookup, per_band, filters)
    s_re, s_im = spectra(got_image, row_lookup, per_band, channels)
    v_full = target.astype(jnp.float32)
    v_re = v_full[:, 0]
    v_im = v_full[:, 1]
    energy = jnp.sum(x_re * x_re + x_im * x_im, axis=1)
    cross_re = jnp.sum(x_re[:, None] * v_re - x_im[:, None] * v_im, axis=2)
    cross_im = jnp.sum(x_re[:, None] * v_im + x_im[:, None] * v_re, axis=2)
    energy, cross_re, cross_im = (
        lax.psum(energy.astype(jnp.bfloat16), "filt").astype(jnp.float32),
        lax.psum(cross_re.astype(jnp.bfloat16), "filt").astype(jnp.float32),
        lax.psum(cross_im.astype(jnp.bfloat16), "filt").astype(jnp.float32),
    )
    denom = penalty + energy[:, None, :]
    coef_re = (s_re - cross_re) / denom
    coef_im = (s_im - cross_im) / denom
    dict_real = v_re + x_re[:, None] * coef_re[:, :, None] + x_im[:, None] * coef_im[:, :, None]
    dict_imag = v_im + x_re[:, None] * coef_im[:, :, None] - x_im[:, None] * coef_re[:, :, None]
    dict_full = jnp.stack([dict_real, dict_imag], axis=1)
    dict_spectra = dict_full.astype(jnp.bfloat16)
    rim_lookup = inverse_rows(height, K)
    folded = jnp.einsum("qpcmg,gty->qpcmty", dict_full, rim_lookup, precision=lax.Precision.HIGHEST)
    rim_real = folded[:, 0, :, :, 0] - folded[:, 1, :, :, 1]
    rim_imag = folded[:, 0, :, :, 1] + folded[:, 1, :, :, 0]
    start_sum = jnp.zeros((filters, channels, K, K), jnp.float32)
    running = start_sum
    pieces = (
        lax.all_gather(rim_real.astype(jnp.bfloat16), "band", axis=0, tiled=True).astype(
            jnp.float32
        ),
        lax.all_gather(rim_imag.astype(jnp.bfloat16), "band", axis=0, tiled=True).astype(
            jnp.float32
        ),
    )
    length = pieces[0].shape[0]
    lookup = inverse_columns(length, width_cols, K)
    running = running + jnp.einsum(
        "qcmy,qx->mcyx", pieces[0], lookup[:, 0], precision=lax.Precision.HIGHEST
    )
    spatial = running - jnp.einsum(
        "qcmy,qx->mcyx", pieces[1], lookup[:, 1], precision=lax.Precision.HIGHEST
    )
    joined = spatial.reshape(filters, channels * K * K) + dual_rim
    spread = jnp.sqrt(jnp.mean(joined * joined, axis=1, keepdims=True))
    dictionary = joined / jnp.maximum(spread, 1.0)
    return (dict_spectra, dictionary)


def solution(mesh):
    placed = (
        P(("grp", "filt"), "band", None),
        P("grp", "band", None),
        P(("grp", "band"), None, None, "filt", None),
        P(("grp", "filt"), None),
    )
    return jax.shard_map(
        body,
        mesh=mesh,
        in_specs=placed,
        out_specs=(P(("grp", "band"), None, None, "filt", None), P(("grp", "filt"), None)),
        check_vma=False,
    )
```

profile of v0, /device:TPU:0, one launch (start us, length us, event | category | flops | bytes accessed | tf_op | source)
XLA Modules:
  0.0 297.8 jit_solution(11534772521772797656)
XLA Ops:
  7.2 0.0 copy-start
  7.2 4.4 %multiply_convert_fusion = (bf16[512,512,1]{1,0,2:T(8,128)(2,1)S(1)}, bf16[512,512,1]{1,0,2:T(8,128)(2,1)S(1)}) fusion(), kind=kLoop, calls=%fused_computation.42 | loop fusion | flops 4980736 | bytes 1048576 | tf_op jit(solution)/shard_map/convert.3
  11.6 0.0 copy-start.5
  11.6 0.1 pad_maximum_fusion.2
  11.7 1.0 copy.59
  12.7 0.4 convert_element_type.110
  13.1 0.0 copy-done.5
  13.1 0.4 fusion.15
  13.5 0.7 copy.69
  14.2 0.6 all_to_all.32
  14.9 0.9 copy.70
  15.7 7.3 %all-to-all-start.1 = ((bf16[8,8,384]{2,0,1:T(8,128)(2,1)}), bf16[8,8,384]{2,0,1:T(8,128)(2,1)S(1)}, u32[]{:S(2)}, u32[]{:S(2)}) async-start(bf16[8,8,384]{2,0,1:T(8,128)(2,1)} %copy.70), calls=%async_computation.1 | async-start | bytes 98304 | tf_op jit(solution)/shard_map/all_to_all | solution.py:71
  23.0 0.0 copy-done
  23.0 0.5 fusion.11
  23.5 1.0 copy.62
  24.5 2.3 all_to_all.28
  26.8 1.1 copy.63
  27.9 1.9 all-to-all-done.1
  29.8 4.1 %all-to-all-start = ((bf16[8,8,4096]{2,0,1:T(8,128)(2,1)}), bf16[8,8,4096]{2,0,1:T(8,128)(2,1)S(1)}, u32[]{:S(2)}, u32[]{:S(2)}) async-start(bf16[8,8,4096]{2,0,1:T(8,128)(2,1)} %copy.63), calls=%async_computation | async-start | bytes 1048576 | tf_op jit(solution)/shard_map/all_to_all | solution.py:70
  33.9 0.0 all-gather.7.cloned.1.call-start
  33.9 0.1 sine_multiply_fusion
  34.0 0.2 multiply_convert_fusion.2
  34.1 6.4 %copy_convert_fusion = f32[64,2,3,32,64]{4,0,3,2,1:T(8,128)} fusion(bf16[64,2,3,32,64]{4,3,2,1,0:T(8,128)(2,1)} %param.6), kind=kLoop, calls=%fused_computation.12 | loop fusion | flops 786432 | bytes 4718592 | tf_op jit(solution)/shard_map/convert_element_type | solution.py:75
  40.5 0.1 copy.71
  40.6 0.1 dot_general.35
  40.7 0.2 fusion.39
  40.9 6.9 %all-to-all-done = bf16[8,8,4096]{2,0,1:T(8,128)(2,1)S(1)} async-done(((bf16[8,8,4096]{2,0,1:T(8,128)(2,1)}), bf16[8,8,4096]{2,0,1:T(8,128)(2,1)S(1)}, u32[]{:S(2)}, u32[]{:S(2)}) %all-to-all-start) | async-done | bytes 524320 | tf_op jit(solution)/shard_map/all_to_all | solution.py:70
  47.9 0.5 copy.64
  48.3 0.0 slice-start
  48.3 0.0 slice-start.1
  48.4 0.9 fusion.22
  49.2 0.7 add_reduce_fusion
  49.9 0.0 copy-start.2
  49.9 0.0 copy-start.3
  49.9 0.6 slice-done
  50.5 1.4 slice-done.1
  51.9 1.1 fusion.4
  53.0 0.0 copy-done.2
  53.0 0.0 copy-done.3
  53.0 3.9 %all-reduce = (bf16[64,3,64]{2,0,1:T(8,128)(2,1)S(1)}, bf16[64,64]{1,0:T(8,128)(2,1)S(1)}, bf16[64,3,64]{2,0,1:T(8,128)(2,1)S(1)}) all-reduce(bf16[64,3,64]{2,0,1:T(8,128)(2,1)S(1)} %get-tuple-element.11, bf16[64,64]{1,0:T(8,128)(2,1)S(1)} %get-tuple-element.17, ...), channel_id=1, replica_groups=mesh['grp'=2,'band'=8,'filt'=2] {'filt'}, use_global_device_ids=true, to_apply=%region_5.6 | all-reduce | flops 28672 | bytes 114688 | tf_op jit(solution)/shard_map/psum | solution.py:84
  57.0 4.5 %multiply_add_fusion = (f32[64,1,3,32,64]{4,0,3,2,1:T(8,128)S(1)}, f32[64,1,3,32,64]{4,0,3,2,1:T(8,128)S(1)}) fusion(f32[64,2,3,32,64]{4,0,3,2,1:T(8,128)} %copy_convert_fusion, f32[64,3,64]{2,0,1:T(8,128)S(1)} %get-tuple-element.25, f32[64,32,64]{2,0,1:T(8,128)} %copy-done.3, f32[64,3,64]{2,0,1:T(8,128)S(1)} %get-tuple-element.24, f32[64,32,64]{2,0,1:T(8,128)} %copy-done.2), kind=kLoop, calls=%fused_computation.14 | loop fusion | flops 3145728 | bytes 7438336 | tf_op jit(solution)/shard_map/add | solution.py:89
  61.5 0.0 copy-start.1
  61.5 17.3 %fusion = f32[64,2,3,32,2,16]{0,5,4,3,2,1:T(8,128)S(1)} fusion(f32[64,1,3,32,64]{4,0,3,2,1:T(8,128)S(1)} %get-tuple-element.21, f32[64,1,3,32,64]{4,0,3,2,1:T(8,128)S(1)} %get-tuple-element.20, f32[64,1,16]{0,2,1:T(8,128)S(1)} %get-tuple-element.30, f32[64,1,16]{0,2,1:T(8,128)S(1)} %get-tuple-element.31), kind=kOutput, calls=%fused_computation.1 | convolution fusion | flops 302778368 | bytes 4726784 | tf_op jit(solution)/shard_map/qpcmg,gty->qpcmty/dot_general | solution.py:94
  78.9 0.0 copy-done.1
  78.9 1.1 fusion.30
  80.0 2.7 copy.77
  82.7 0.0 all-gather.7.cloned.1.call-update
  82.7 0.3 all-gather.5.cloned.1.call-start
  83.0 2.7 copy.75
  85.7 0.0 all-gather.5.cloned.1.call-update
  85.7 2.4 fusion.2
  88.1 3.7 %copy.80 = bf16[64,2,3,32,64]{4,3,2,1,0:T(8,128)(2,1)} copy(bf16[64,2,3,32,64]{4,0,3,2,1:T(8,128)(2,1)S(1)} %fusion.2) | data formatting | bytes 3145728
  91.7 89.3 %all-gather.7.cloned.1.call-done = bf16[512,1,3,32,1,16]{3,5,4,2,1,0:T(8,128)(2,1)} async-done(((bf16[64,1,3,32,1,16]{3,5,4,2,1,0:T(8,128)(2,1)}), bf16[512,1,3,32,1,16]{3,5,4,2,1,0:T(8,128)(2,1)}) %all-gather.7.cloned.1.call-update) | async-done | bytes 1572880 | tf_op jit(solution)/shard_map/all_gather | solution.py:103
  181.0 6.4 %copy.78 = bf16[512,1,3,32,1,16]{0,3,5,2,4,1:T(8,128)(2,1)S(1)} copy(bf16[512,1,3,32,1,16]{3,5,4,2,1,0:T(8,128)(2,1)} %all-gather.7.cloned.1.call-done) | data formatting | bytes 3145728 | tf_op jit(solution)/shard_map/all_gather | solution.py:103
  187.4 3.2 %fusion.7 = f32[16,3,32,16]{2,0,3,1:T(8,128)S(1)} fusion(bf16[512,1,3,32,1,16]{0,3,5,2,4,1:T(8,128)(2,1)S(1)} %copy.78), kind=kOutput, calls=%fused_computation.15 | convolution fusion | flops 151117824 | bytes 1671168 | tf_op jit(solution)/shard_map/qcmy,qx->mcyx/dot_general | solution.py:112
  190.5 0.0 copy-start.4
  190.5 89.9 %all-gather.5.cloned.1.call-done = bf16[512,1,3,32,1,16]{3,5,4,2,1,0:T(8,128)(2,1)} async-done(((bf16[64,1,3,32,1,16]{3,5,4,2,1,0:T(8,128)(2,1)}), bf16[512,1,3,32,1,16]{3,5,4,2,1,0:T(8,128)(2,1)}) %all-gather.5.cloned.1.call-update) | async-done | bytes 1572880 | tf_op jit(solution)/shard_map/all_gather | solution.py:100
  280.4 6.4 %copy.76 = bf16[512,1,3,32,1,16]{0,3,5,2,4,1:T(8,128)(2,1)S(1)} copy(bf16[512,1,3,32,1,16]{3,5,4,2,1,0:T(8,128)(2,1)} %all-gather.5.cloned.1.call-done) | data formatting | bytes 3145728 | tf_op jit(solution)/shard_map/all_gather | solution.py:100
  286.8 3.2 %fusion.12 = f32[16,3,32,16]{2,0,3,1:T(8,128)S(1)} fusion(f32[16,3,32,16]{2,0,3,1:T(8,128)S(1)} %fusion.7, bf16[512,1,3,32,1,16]{0,3,5,2,4,1:T(8,128)(2,1)S(1)} %copy.76), kind=kOutput, calls=%fused_computation.24 | convolution fusion | flops 151142400 | bytes 1769472 | tf_op jit(solution)/shard_map/qcmy,qx->mcyx/dot_general | solution.py:109
  290.0 0.2 copy.79
  290.1 0.0 copy-done.4
  290.1 0.1 multiply_reduce_fusion
  290.3 0.7 broadcast_divide_fusion
  (4 shorter events, 0.1 us)
Async XLA Ops:
  7.2 15.8 %copy-start = (bf16[32,8,512]{2,1,0:T(8,128)(2,1)S(1)}, bf16[32,8,512]{2,1,0:T(8,128)(2,1)}, u32[]{:S(2)}) copy-start(bf16[32,8,512]{2,1,0:T(8,128)(2,1)} %param.4) | copy-start | bytes 786436
  11.6 1.6 copy-start.5
  15.7 14.0 %all-to-all-start.1 = ((bf16[8,8,384]{2,0,1:T(8,128)(2,1)}), bf16[8,8,384]{2,0,1:T(8,128)(2,1)S(1)}, u32[]{:S(2)}, u32[]{:S(2)}) async-start(bf16[8,8,384]{2,0,1:T(8,128)(2,1)} %copy.70), calls=%async_computation.1 | async-start | bytes 98304 | tf_op jit(solution)/shard_map/all_to_all | solution.py:71
  29.8 18.1 %all-to-all-start = ((bf16[8,8,4096]{2,0,1:T(8,128)(2,1)}), bf16[8,8,4096]{2,0,1:T(8,128)(2,1)S(1)}, u32[]{:S(2)}, u32[]{:S(2)}) async-start(bf16[8,8,4096]{2,0,1:T(8,128)(2,1)} %copy.63), calls=%async_computation | async-start | bytes 1048576 | tf_op jit(solution)/shard_map/all_to_all | solution.py:70
  33.9 147.1 %all-gather.7.cloned.1.call-start = ((), (), s32[]{:S(2)}) async-start(), calls=%async_computation.3 | async-start | bytes 7077888 | tf_op jit(solution)/shard_map/all_gather | solution.py:103
  48.3 2.2 slice-start
  48.3 3.6 %slice-start.1 = ((s8[6291456]{0:T(1024)(128)(4,1)}), s8[2097152]{0:T(1024)(128)(4,1)S(1)}, s32[]{:S(2)}) async-start(s8[6291456]{0:T(1024)(128)(4,1)} %bitcast.128), calls=%async_computation.5 | async-start | bytes 4194304
  49.9 3.1 %copy-start.2 = (f32[64,32,64]{2,0,1:T(8,128)}, f32[64,32,64]{2,0,1:T(8,128)S(1)}, u32[]{:S(2)}) copy-start(f32[64,32,64]{2,0,1:T(8,128)S(1)} %get-tuple-element.18) | copy-start | bytes 1572868
  49.9 3.1 %copy-start.3 = (f32[64,32,64]{2,0,1:T(8,128)}, f32[64,32,64]{2,0,1:T(8,128)S(1)}, u32[]{:S(2)}) copy-start(f32[64,32,64]{2,0,1:T(8,128)S(1)} %get-tuple-element.19) | copy-start | bytes 1572868
  61.5 17.4 %copy-start.1 = (f32[64,1,3,32,64]{4,0,3,2,1:T(8,128)}, f32[64,1,3,32,64]{4,0,3,2,1:T(8,128)S(1)}, u32[]{:S(2)}) copy-start(f32[64,1,3,32,64]{4,0,3,2,1:T(8,128)S(1)} %get-tuple-element.21) | copy-start | bytes 4718596
  82.7 197.7 %all-gather.5.cloned.1.call-start = ((), (), s32[]{:S(2)}) async-start(), calls=%async_computation.2 | async-start | bytes 7077888 | tf_op jit(solution)/shard_map/all_gather | solution.py:100
  190.5 99.6 %copy-start.4 = (f32[32,768]{1,0:T(8,128)S(1)}, f32[32,768]{1,0:T(8,128)}, u32[]{:S(2)}) copy-start(f32[32,768]{1,0:T(8,128)} %param.7) | copy-start | bytes 294916
Sparse Core Ops, SparseCore 0:
  82.9 98.1 all-gather.6
  183.2 97.1 all-gather.4
where the time goes:
time: 298 us
  waiting for transfers between devices  188 us (63%)
  local copies, waits for them, and re-layouts  32.7 us (11%)
  matrix products  25.6 us (9%)
  other arithmetic  21.7 us (7%)
  between operations  14.3 us (5%)
  starting transfers between devices  11.6 us (4%)
  blocking collectives  3.9 us (1%)
    all_gather x1, waiting for transfers between devices, body(): lax.all_gather(rim_real.astype(jnp.bfloat16), 'band', axis=0, tiled=True)  89.9 us
    all_gather x1, waiting for transfers between devices, body(): lax.all_gather(rim_imag.astype(jnp.bfloat16), 'band', axis=0, tiled=True)  89.3 us
    dot_general x1, matrix products, body(): jnp.einsum('qpcmg,gty->qpcmty', dict_full, rim_lookup, precision=lax.Prec...  17.3 us
    all_to_all x1, starting transfers between devices, body(): lax.all_to_all(col_image, 'band', split_axis=1, concat_axis=0, tiled=True)  7.25 us
    all_to_all x1, waiting for transfers between devices, body(): lax.all_to_all(col_maps, 'band', split_axis=1, concat_axis=0, tiled=True)  6.91 us
    convert_element_type x1, other arithmetic, body(): v_full = target.astype(jnp.float32)  6.37 us
    all_gather x1, local copies, waits for them, and re-layouts, body(): lax.all_gather(rim_imag.astype(jnp.bfloat16), 'band', axis=0, tiled=True)  6.36 us
    all_gather x1, local copies, waits for them, and re-layouts, body(): lax.all_gather(rim_real.astype(jnp.bfloat16), 'band', axis=0, tiled=True)  6.36 us
  transfers between devices with their start and end apart: 4, of which 4 were waited for; matrix products, arithmetic and copies ran while one was open for 9% of the time, Pallas kernels for 0%

commit v1 on v0

--- a/solution.py
+++ b/solution.py
@@ -55,6 +55,23 @@
 
 
 def body(coeff_maps, image, target, dual_rim):
+
+    def _group_windows(panel, axis_k):
+        side_arr = jax.lax.axis_size("band")
+        block_out = jax.lax.axis_index("band")
+        s_next, res = (side_arr, block_out)
+        state_now, v_now = (panel, 1)
+        while v_now < s_next:
+            known = range(s_next)
+            f_next = map(lambda to_i: (to_i, to_i ^ v_now), known)
+            mid_arr = list(f_next)
+            mat_out = jax.lax.ppermute(state_now, axis_name="band", perm=mid_arr)
+            after = jnp.concatenate([state_now, mat_out], axis=axis_k)
+            work_now = jnp.concatenate([mat_out, state_now], axis=axis_k)
+            state_now = jnp.where(res & v_now == 0, after, work_now)
+            v_now = 2 * v_now
+        return state_now
+
     filters, band_rows, width_cols = coeff_maps.shape
     channels = image.shape[0]
     band_count = lax.axis_size("band")
@@ -100,9 +117,7 @@
         lax.all_gather(rim_real.astype(jnp.bfloat16), "band", axis=0, tiled=True).astype(
             jnp.float32
         ),
-        lax.all_gather(rim_imag.astype(jnp.bfloat16), "band", axis=0, tiled=True).astype(
-            jnp.float32
-        ),
+        _group_windows(rim_imag.astype(jnp.bfloat16), 0).astype(jnp.float32),
     )
     length = pieces[0].shape[0]
     lookup = inverse_columns(length, width_cols, K)

time: 298 us -> 238 us (0.80)
  waiting for transfers between devices: 188 us -> 127 us
  local copies, waits for them, and re-layouts: 32.7 us -> 23.6 us
  other arithmetic: 21.7 us -> 29.5 us
    ppermute x0 -> x3, waiting for transfers between devices: none -> 112 us  [_group_windows(): mat_out = jax.lax.ppermute(state_now, axis_name='band', perm=mid_arr)]
    all_gather x1 -> x0, waiting for transfers between devices: 89.3 us -> none  [body(): lax.all_gather(rim_imag.astype(jnp.bfloat16), 'band', axis=0, tiled=True)]
    all_gather x1, waiting for transfers between devices: 89.9 us -> 6.2 us  [body(): lax.all_gather(rim_real.astype(jnp.bfloat16), 'band', axis=0, tiled=True)]
    select_n x0 -> x3, other arithmetic: none -> 7.67 us  [_group_windows(): state_now = jnp.where(res & v_now == 0, after, work_now)]
    all_gather x1 -> x0, local copies, waits for them, and re-layouts: 6.36 us -> none  [body(): lax.all_gather(rim_imag.astype(jnp.bfloat16), 'band', axis=0, tiled=True)]
  transfers between devices with their start and end apart: 4 -> 6, of which waited for: 4 -> 6; matrix products, arithmetic and copies ran while one was open for 9% -> 10% of each run, Pallas kernels for 0% -> 0%
where the time goes in v1:
time: 238 us; the launch traced here: 237 us
  waiting for transfers between devices  127 us (53%)
  other arithmetic  29.5 us (12%)
  matrix products  25.8 us (11%)
  local copies, waits for them, and re-layouts  23.6 us (10%)
  between operations  14.3 us (6%)
  starting transfers between devices  12.9 us (5%)
  blocking collectives  3.9 us (2%)
    ppermute x3, waiting for transfers between devices, _group_windows(): mat_out = jax.lax.ppermute(state_now, axis_name='band', perm=mid_arr)  112 us
    dot_general x1, matrix products, body(): jnp.einsum('qpcmg,gty->qpcmty', dict_full, rim_lookup, precision=lax.Prec...  17.3 us
    select_n x3, other arithmetic, _group_windows(): state_now = jnp.where(res & v_now == 0, after, work_now)  7.67 us
    all_to_all x1, starting transfers between devices, body(): lax.all_to_all(col_image, 'band', split_axis=1, concat_axis=0, tiled=True)  7.25 us
    all_to_all x1, waiting for transfers between devices, body(): lax.all_to_all(col_maps, 'band', split_axis=1, concat_axis=0, tiled=True)  6.91 us
    convert_element_type x1, other arithmetic, body(): v_full = target.astype(jnp.float32)  6.37 us
    all_gather x1, local copies, waits for them, and re-layouts, body(): lax.all_gather(rim_real.astype(jnp.bfloat16), 'band', axis=0, tiled=True)  6.36 us
    all_gather x1, waiting for transfers between devices, body(): lax.all_gather(rim_real.astype(jnp.bfloat16), 'band', axis=0, tiled=True)  6.2 us
  transfers between devices with their start and end apart: 6, of which 6 were waited for; matrix products, arithmetic and copies ran while one was open for 10% of the time, Pallas kernels for 0%

profile of v1, /device:TPU:0, one launch (start us, length us, event | category | flops | bytes accessed | tf_op | source)
XLA Modules:
  0.0 237.4 jit_solution(510654567191855901)
XLA Ops:
  7.2 0.0 copy-start
  7.2 4.4 %multiply_convert_fusion = (bf16[512,512,1]{1,0,2:T(8,128)(2,1)S(1)}, bf16[512,512,1]{1,0,2:T(8,128)(2,1)S(1)}) fusion(), kind=kLoop, calls=%fused_computation.43 | loop fusion | flops 4980736 | bytes 1048576 | tf_op jit(solution)/shard_map/convert.3
  11.6 0.0 copy-start.5
  11.6 0.1 pad_maximum_fusion.2
  11.7 1.0 copy.58
  12.7 0.4 convert_element_type.110
  13.1 0.0 copy-done.5
  13.1 0.4 fusion.15
  13.5 0.7 copy.68
  14.2 0.6 all_to_all.32
  14.9 0.9 copy.69
  15.7 7.3 %all-to-all-start.1 = ((bf16[8,8,384]{2,0,1:T(8,128)(2,1)}), bf16[8,8,384]{2,0,1:T(8,128)(2,1)S(1)}, u32[]{:S(2)}, u32[]{:S(2)}) async-start(bf16[8,8,384]{2,0,1:T(8,128)(2,1)} %copy.69), calls=%async_computation.1 | async-start | bytes 98304 | tf_op jit(solution)/shard_map/all_to_all | solution.py:88
  23.0 0.0 copy-done
  23.0 0.5 fusion.11
  23.5 1.0 copy.61
  24.5 2.3 all_to_all.28
  26.8 1.1 copy.62
  27.9 1.9 all-to-all-done.1
  29.8 4.1 %all-to-all-start = ((bf16[8,8,4096]{2,0,1:T(8,128)(2,1)}), bf16[8,8,4096]{2,0,1:T(8,128)(2,1)S(1)}, u32[]{:S(2)}, u32[]{:S(2)}) async-start(bf16[8,8,4096]{2,0,1:T(8,128)(2,1)} %copy.62), calls=%async_computation | async-start | bytes 1048576 | tf_op jit(solution)/shard_map/all_to_all | solution.py:87
  33.9 0.0 all-gather.3.cloned.1.call-start
  33.9 0.1 sine_multiply_fusion
  34.0 0.2 multiply_convert_fusion.2
  34.1 6.4 %copy_convert_fusion = f32[64,2,3,32,64]{4,0,3,2,1:T(8,128)} fusion(bf16[64,2,3,32,64]{4,3,2,1,0:T(8,128)(2,1)} %param.6), kind=kLoop, calls=%fused_computation.12 | loop fusion | flops 786432 | bytes 4718592 | tf_op jit(solution)/shard_map/convert_element_type | solution.py:92
  40.5 0.1 copy.70
  40.6 0.1 dot_general.35
  40.7 0.2 fusion.40
  40.9 6.9 %all-to-all-done = bf16[8,8,4096]{2,0,1:T(8,128)(2,1)S(1)} async-done(((bf16[8,8,4096]{2,0,1:T(8,128)(2,1)}), bf16[8,8,4096]{2,0,1:T(8,128)(2,1)S(1)}, u32[]{:S(2)}, u32[]{:S(2)}) %all-to-all-start) | async-done | bytes 524320 | tf_op jit(solution)/shard_map/all_to_all | solution.py:87
  47.9 0.5 copy.63
  48.3 0.0 slice-start
  48.3 0.0 slice-start.1
  48.4 0.9 fusion.22
  49.2 0.7 add_reduce_fusion
  49.9 0.0 copy-start.2
  49.9 0.0 copy-start.3
  49.9 0.6 slice-done
  50.5 1.4 slice-done.1
  51.9 1.1 fusion.4
  53.0 0.0 copy-done.2
  53.0 3.9 %all-reduce = (bf16[64,3,64]{2,0,1:T(8,128)(2,1)S(1)}, bf16[64,64]{1,0:T(8,128)(2,1)S(1)}, bf16[64,3,64]{2,0,1:T(8,128)(2,1)S(1)}) all-reduce(bf16[64,3,64]{2,0,1:T(8,128)(2,1)S(1)} %get-tuple-element.11, bf16[64,64]{1,0:T(8,128)(2,1)S(1)} %get-tuple-element.17, ...), channel_id=1, replica_groups=mesh['grp'=2,'band'=8,'filt'=2] {'filt'}, use_global_device_ids=true, to_apply=%region_5.6 | all-reduce | flops 28672 | bytes 114688 | tf_op jit(solution)/shard_map/psum | solution.py:101
  57.0 4.5 %multiply_add_fusion = (f32[64,1,3,32,64]{4,0,3,2,1:T(8,128)S(1)}, f32[64,1,3,32,64]{4,0,3,2,1:T(8,128)S(1)}) fusion(f32[64,2,3,32,64]{4,0,3,2,1:T(8,128)} %copy_convert_fusion, f32[64,3,64]{2,0,1:T(8,128)S(1)} %get-tuple-element.25, f32[64,32,64]{2,0,1:T(8,128)} %copy-done.3, f32[64,3,64]{2,0,1:T(8,128)S(1)} %get-tuple-element.24, f32[64,32,64]{2,0,1:T(8,128)} %copy-done.2), kind=kLoop, calls=%fused_computation.14 | loop fusion | flops 3145728 | bytes 7438336 | tf_op jit(solution)/shard_map/add | solution.py:106
  61.5 0.0 copy-start.1
  61.5 17.3 %fusion = f32[64,2,3,32,2,16]{0,5,4,3,2,1:T(8,128)S(1)} fusion(f32[64,1,3,32,64]{4,0,3,2,1:T(8,128)S(1)} %get-tuple-element.21, f32[64,1,3,32,64]{4,0,3,2,1:T(8,128)S(1)} %get-tuple-element.20, f32[64,1,16]{0,2,1:T(8,128)S(1)} %get-tuple-element.30, f32[64,1,16]{0,2,1:T(8,128)S(1)} %get-tuple-element.31), kind=kOutput, calls=%fused_computation.1 | convolution fusion | flops 302778368 | bytes 4726784 | tf_op jit(solution)/shard_map/qpcmg,gty->qpcmty/dot_general | solution.py:111
  78.9 0.0 copy-done.1
  78.9 1.1 fusion.31
  79.9 2.7 %copy.74 = bf16[64,1,3,32,1,16]{3,5,4,2,1,0:T(8,128)(2,1)} copy(bf16[64,1,3,32,1,16]{0,5,4,3,2,1:T(8,128)(2,1)} %get-tuple-element.23) | data formatting | bytes 393216 | tf_op jit(solution)/shard_map/convert_element_type | solution.py:117
  82.6 0.0 all-gather.3.cloned.1.call-update
  82.6 1.5 collective-permute-start
  84.1 12.2 %collective-permute-done = bf16[64,3,32,16]{0,3,2,1:T(8,128)(2,1)} collective-permute-done((bf16[64,3,32,16]{0,3,2,1:T(8,128)(2,1)}, bf16[64,3,32,16]{0,3,2,1:T(8,128)(2,1)}, u32[]{:S(2)}, u32[]{:S(2)}) %collective-permute-start) | collective-permute-done | bytes 196640 | tf_op jit(solution)/shard_map/ppermute | solution.py:68
  96.4 2.6 %maximum_select_fusion.2 = bf16[128,3,32,16]{0,3,2,1:T(8,128)(2,1)} fusion(bf16[64,3,32,16]{0,3,2,1:T(8,128)(2,1)} %collective-permute-done, bf16[64,3,32,16]{0,3,2,1:T(8,128)(2,1)} %get-tuple-element.22, pred[]{:T(512)S(6)} %eq.19), kind=kLoop, calls=%fused_computation.54 | loop fusion | flops 1769472 | bytes 786433 | tf_op jit(solution)/shard_map/jit(_where)/select_n | solution.py:71
  98.9 0.0 collective-permute-start.1
  98.9 27.9 %collective-permute-done.1 = bf16[128,3,32,16]{0,3,2,1:T(8,128)(2,1)} collective-permute-done((bf16[128,3,32,16]{0,3,2,1:T(8,128)(2,1)}, bf16[128,3,32,16]{0,3,2,1:T(8,128)(2,1)}, u32[]{:S(2)}, u32[]{:S(2)}) %collective-permute-start.1) | collective-permute-done | bytes 393248 | tf_op jit(solution)/shard_map/ppermute | solution.py:68
  126.9 2.5 %maximum_select_fusion.1 = bf16[256,3,32,16]{0,3,2,1:T(8,128)(2,1)} fusion(bf16[128,3,32,16]{0,3,2,1:T(8,128)(2,1)} %collective-permute-done.1, bf16[128,3,32,16]{0,3,2,1:T(8,128)(2,1)} %maximum_select_fusion.2, pred[]{:T(512)S(6)} %eq.18), kind=kLoop, calls=%fused_computation.52 | loop fusion | flops 3538944 | bytes 1572865 | tf_op jit(solution)/shard_map/jit(_where)/select_n | solution.py:71
  129.4 0.0 collective-permute-start.2
  129.4 2.6 %fusion.2 = bf16[64,2,3,32,64]{4,0,3,2,1:T(8,128)(2,1)S(1)} fusion(f32[64,1,3,32,64]{4,0,3,2,1:T(8,128)} %copy-done.1, f32[64,1,3,32,64]{4,0,3,2,1:T(8,128)S(1)} %get-tuple-element.20), kind=kLoop, calls=%fused_computation.3 | loop fusion | flops 786432 | bytes 4718592 | tf_op jit(solution)/shard_map/convert_element_type | solution.py:109
  132.0 3.7 %copy.78 = bf16[64,2,3,32,64]{4,3,2,1,0:T(8,128)(2,1)} copy(bf16[64,2,3,32,64]{4,0,3,2,1:T(8,128)(2,1)S(1)} %fusion.2) | data formatting | bytes 3145728
  135.7 72.2 %collective-permute-done.2 = bf16[256,3,32,16]{0,3,2,1:T(8,128)(2,1)} collective-permute-done((bf16[256,3,32,16]{0,3,2,1:T(8,128)(2,1)}, bf16[256,3,32,16]{0,3,2,1:T(8,128)(2,1)}, u32[]{:S(2)}, u32[]{:S(2)}) %collective-permute-start.2) | collective-permute-done | bytes 786464 | tf_op jit(solution)/shard_map/ppermute | solution.py:68
  207.8 2.6 %maximum_select_fusion = bf16[512,3,32,16]{0,3,2,1:T(8,128)(2,1)S(1)} fusion(bf16[256,3,32,16]{0,3,2,1:T(8,128)(2,1)} %collective-permute-done.2, bf16[256,3,32,16]{0,3,2,1:T(8,128)(2,1)} %maximum_select_fusion.1, pred[]{:T(512)S(6)} %eq.17), kind=kLoop, calls=%fused_computation.15 | loop fusion | flops 7077888 | bytes 3145729 | tf_op jit(solution)/shard_map/jit(_where)/select_n | solution.py:71
  210.4 6.2 %all-gather.3.cloned.1.call-done = bf16[512,1,3,32,1,16]{3,5,4,2,1,0:T(8,128)(2,1)} async-done(((bf16[64,1,3,32,1,16]{3,5,4,2,1,0:T(8,128)(2,1)}), bf16[512,1,3,32,1,16]{3,5,4,2,1,0:T(8,128)(2,1)}) %all-gather.3.cloned.1.call-update) | async-done | bytes 1572880 | tf_op jit(solution)/shard_map/all_gather | solution.py:117
  216.6 6.4 %copy.75 = bf16[512,1,3,32,1,16]{0,3,5,2,4,1:T(8,128)(2,1)S(1)} copy(bf16[512,1,3,32,1,16]{3,5,4,2,1,0:T(8,128)(2,1)} %all-gather.3.cloned.1.call-done) | data formatting | bytes 3145728 | tf_op jit(solution)/shard_map/all_gather | solution.py:117
  223.0 3.2 %fusion.7 = f32[16,3,32,16]{2,0,3,1:T(8,128)S(1)} fusion(bf16[512,1,3,32,1,16]{0,3,5,2,4,1:T(8,128)(2,1)S(1)} %copy.75), kind=kOutput, calls=%fused_computation.16 | convolution fusion | flops 151117824 | bytes 1671168 | tf_op jit(solution)/shard_map/qcmy,qx->mcyx/dot_general | solution.py:124
  226.2 3.3 %fusion.12 = f32[16,3,32,16]{2,0,3,1:T(8,128)S(1)} fusion(f32[16,3,32,16]{2,0,3,1:T(8,128)S(1)} %fusion.7, bf16[512,3,32,16]{0,3,2,1:T(8,128)(2,1)S(1)} %maximum_select_fusion), kind=kOutput, calls=%fused_computation.25 | convolution fusion | flops 151142400 | bytes 1769472 | tf_op jit(solution)/shard_map/qcmy,qx->mcyx/dot_general | solution.py:127
  229.5 0.2 copy.77
  229.6 0.1 multiply_reduce_fusion
  229.8 0.7 broadcast_divide_fusion
  (7 shorter events, 0.1 us)
Async XLA Ops:
  7.2 15.8 %copy-start = (bf16[32,8,512]{2,1,0:T(8,128)(2,1)S(1)}, bf16[32,8,512]{2,1,0:T(8,128)(2,1)}, u32[]{:S(2)}) copy-start(bf16[32,8,512]{2,1,0:T(8,128)(2,1)} %param.4) | copy-start | bytes 786436
  11.6 1.6 copy-start.5
  15.7 14.0 %all-to-all-start.1 = ((bf16[8,8,384]{2,0,1:T(8,128)(2,1)}), bf16[8,8,384]{2,0,1:T(8,128)(2,1)S(1)}, u32[]{:S(2)}, u32[]{:S(2)}) async-start(bf16[8,8,384]{2,0,1:T(8,128)(2,1)} %copy.69), calls=%async_computation.1 | async-start | bytes 98304 | tf_op jit(solution)/shard_map/all_to_all | solution.py:88
  29.8 18.1 %all-to-all-start = ((bf16[8,8,4096]{2,0,1:T(8,128)(2,1)}), bf16[8,8,4096]{2,0,1:T(8,128)(2,1)S(1)}, u32[]{:S(2)}, u32[]{:S(2)}) async-start(bf16[8,8,4096]{2,0,1:T(8,128)(2,1)} %copy.62), calls=%async_computation | async-start | bytes 1048576 | tf_op jit(solution)/shard_map/all_to_all | solution.py:87
  33.9 182.8 %all-gather.3.cloned.1.call-start = ((), (), s32[]{:S(2)}) async-start(), calls=%async_computation.2 | async-start | bytes 7077888 | tf_op jit(solution)/shard_map/all_gather | solution.py:117
  48.3 2.2 slice-start
  48.3 3.6 %slice-start.1 = ((s8[6291456]{0:T(1024)(128)(4,1)}), s8[2097152]{0:T(1024)(128)(4,1)S(1)}, s32[]{:S(2)}) async-start(s8[6291456]{0:T(1024)(128)(4,1)} %bitcast.125), calls=%async_computation.4 | async-start | bytes 4194304
  49.9 3.1 %copy-start.2 = (f32[64,32,64]{2,0,1:T(8,128)}, f32[64,32,64]{2,0,1:T(8,128)S(1)}, u32[]{:S(2)}) copy-start(f32[64,32,64]{2,0,1:T(8,128)S(1)} %get-tuple-element.18) | copy-start | bytes 1572868
  49.9 3.1 %copy-start.3 = (f32[64,32,64]{2,0,1:T(8,128)}, f32[64,32,64]{2,0,1:T(8,128)S(1)}, u32[]{:S(2)}) copy-start(f32[64,32,64]{2,0,1:T(8,128)S(1)} %get-tuple-element.19) | copy-start | bytes 1572868
  61.5 17.4 %copy-start.1 = (f32[64,1,3,32,64]{4,0,3,2,1:T(8,128)}, f32[64,1,3,32,64]{4,0,3,2,1:T(8,128)S(1)}, u32[]{:S(2)}) copy-start(f32[64,1,3,32,64]{4,0,3,2,1:T(8,128)S(1)} %get-tuple-element.21) | copy-start | bytes 4718596
  82.6 13.7 %collective-permute-start = (bf16[64,3,32,16]{0,3,2,1:T(8,128)(2,1)}, bf16[64,3,32,16]{0,3,2,1:T(8,128)(2,1)}, u32[]{:S(2)}, u32[]{:S(2)}) collective-permute-start(bf16[64,3,32,16]{0,3,2,1:T(8,128)(2,1)} %get-tuple-element.22), channel_id=1, source_target_pairs={{0,2},{2,0},{4,6},{6,4},{8,10},{10,8},{12,14},{14,12},{1,3},{3,1},... | collective-permute-start | bytes 589832 | tf_op jit(solution)/shard_map/ppermute | solution.py:68
  98.9 27.9 %collective-permute-start.1 = (bf16[128,3,32,16]{0,3,2,1:T(8,128)(2,1)}, bf16[128,3,32,16]{0,3,2,1:T(8,128)(2,1)}, u32[]{:S(2)}, u32[]{:S(2)}) collective-permute-start(bf16[128,3,32,16]{0,3,2,1:T(8,128)(2,1)} %maximum_select_fusion.2), channel_id=1, source_target_pairs={{0,4},{2,6},{4,0},{6,2},{8,12},{10,14},{12,8},{14,10},{1,5},{3,7},... | collective-permute-start | bytes 1179656 | tf_op jit(solution)/shard_map/ppermute | solution.py:68
  129.4 78.5 %collective-permute-start.2 = (bf16[256,3,32,16]{0,3,2,1:T(8,128)(2,1)}, bf16[256,3,32,16]{0,3,2,1:T(8,128)(2,1)}, u32[]{:S(2)}, u32[]{:S(2)}) collective-permute-start(bf16[256,3,32,16]{0,3,2,1:T(8,128)(2,1)} %maximum_select_fusion.1), channel_id=1, source_target_pairs={{0,8},{2,10},{4,12},{6,14},{8,0},{10,2},{12,4},{14,6},{1,9},{3,11}... | collective-permute-start | bytes 2359304 | tf_op jit(solution)/shard_map/ppermute | solution.py:68
  223.0 6.6 %copy-start.4 = (f32[32,768]{1,0:T(8,128)S(1)}, f32[32,768]{1,0:T(8,128)}, u32[]{:S(2)}) copy-start(f32[32,768]{1,0:T(8,128)} %param.7) | copy-start | bytes 294916
Sparse Core Ops, SparseCore 0:
  82.8 133.8 all-gather.2
